TPU v7x, 32 devices: a whole 2x2x4 slice. The times are simulated.
32 devices in a mesh: section: 4 (over y, core), space: 8 (over z, x).
Axes of the slice: x: 2, y: 2, z: 4, core: 2. Of those that a mesh axis runs over, the one named last changes fastest.
Arguments:
- features: bfloat16 [4, 2048, 256], P('section', 'space'), may hold values from -6 to 6
- out_grad: bfloat16 [4, 2048, 256], P('section', 'space'), may hold values from -6 to 6
- weight: bfloat16 [4, 27, 256, 256], P('section'), may hold values from -0.078125 to 0.078125
- counts: int32 [4, 16], P('section', 'space'), may hold values from 16 to 128
- local_rows: int32 [4, 27, 2048], P('section', None, 'space'), may hold values from -1 to 255, as said below
- send_rows: int32 [4, 8, 27, 8, 2], P('section', 'space'), may hold values from -1 to 255, as said below
- recv_rows: int32 [4, 8, 27, 8, 2], P('section', 'space'), may hold values from -1 to 255, as said below
Outputs:
- handoff: bfloat16 [4, 2048, 256], P('section', 'space')
- weight_grad: float32 [4, 6912, 256], P('section', 'space')
Inputs may be any that keep to these rules, and one draw needn't show every extreme that they name: `local_rows`: -1 where a voxel has no pair on its own device at that offset. `send_rows`: for each offset and two different devices, the first 1 to 2 slots are used and the rest are -1; a device's slots to itself are all -1; for every sending device there is one offset at which all 2 slots to every other device are used. `recv_rows`: slot for slot the pairs of send_rows seen from the receiving device, -1 in the same empty slots.
All inputs are finite; a program needn't handle non-finite values.
Results may differ from a plain program's by a relative error of at most 0.0019.
Values may be sent and summed in bfloat16 or wider, within the bound.
No kernel may reach another device: no remote copies, remote signals or barrier semaphores. Data moves between devices by JAX's collectives and lax.ppermute only.
A program may use at most 64 MiB of HBM per device.

v0:
```python
import jax
import jax.numpy as jnp
from jax import lax
from jax.sharding import PartitionSpec as P

BLOCK = 128


def from_behind(block, axis, distance):
    devices = range(lax.axis_size(axis))
    route = [(i - distance, i) for i in devices if i - distance in devices]
    return lax.ppermute(block, axis, route)


def take_rows(source, row_index, nothing):
    picked = jnp.take(source, jnp.maximum(row_index, 0), axis=0)
    return jnp.where((row_index >= 0)[..., None], picked, nothing)


def body(features, out_grad, weight, counts, local_rows, send_rows, recv_rows):
    inputs = features[0]
    gradient = out_grad[0]
    kernel = weight[0]
    rows_dev = inputs.shape[0]
    channels = inputs.shape[1]
    offsets = kernel.shape[0]
    inside = (jnp.arange(BLOCK, dtype=jnp.int32)[None, :] < counts[0][:, None]).reshape(rows_dev, 1)
    nothing = jnp.zeros((), inputs.dtype)
    xmask = jnp.where(inside, inputs, nothing)
    gmask = jnp.where(inside, gradient, nothing)
    local_map = local_rows[0].T
    gathered = take_rows(gmask, local_map, nothing)
    input_grad = lax.dot_general(
        gathered, kernel, (((1, 2), (0, 1)), ((), ())), preferred_element_type=jnp.float32
    )
    weight_grad = lax.dot_general(
        gathered, xmask, (((0,), (0,)), ((), ())), preferred_element_type=jnp.float32
    )
    send_map = send_rows[0, 0]
    recv_map = recv_rows[0, 0]
    flat_shape = (offsets, -1, channels)
    outgoing = take_rows(gmask, send_map, nothing)
    partial_value = (
        lax.dot_general(
            outgoing.reshape(flat_shape),
            kernel,
            (((2,), (1,)), ((0,), (0,))),
            preferred_element_type=jnp.float32,
        )
        .astype(jnp.bfloat16)
        .reshape(outgoing.shape)
    )
    arrived = lax.all_to_all(partial_value, "space", split_axis=1, concat_axis=1, tiled=True)
    returned = lax.all_to_all(
        take_rows(xmask, recv_map, nothing), "space", split_axis=1, concat_axis=1, tiled=True
    )
    weight_grad = weight_grad + lax.dot_general(
        outgoing.reshape(flat_shape),
        returned.reshape(flat_shape),
        (((1,), (1,)), ((0,), (0,))),
        preferred_element_type=jnp.float32,
    )
    incoming = arrived.reshape(-1, channels).astype(jnp.float32)
    target = jnp.where(recv_map >= 0, recv_map, rows_dev).reshape(-1)
    input_grad = input_grad.at[target].add(incoming, mode="drop")
    result = jnp.where(inside, input_grad, 0.0).astype(jnp.bfloat16)
    handoff = from_behind(result, "section", -1)
    loss_scale = float(rows_dev * lax.axis_size("space")) ** (-0.5)
    summed = lax.psum_scatter(
        (weight_grad * loss_scale).reshape(offsets * channels, channels),
        "space",
        scatter_dimension=0,
        tiled=True,
    )
    return (handoff[None], summed[None])


def solution(mesh):
    placed = (
        P("section", "space", None),
        P("section", "space", None),
        P("section", None, None, None),
        P("section", "space"),
        P("section", None, "space"),
        P("section", "space", None, None, None),
        P("section", "space", None, None, None),
    )
    return jax.shard_map(
        body,
        mesh=mesh,
        in_specs=placed,
        out_specs=(P("section", "space", None), P("section", "space", None)),
        check_vma=False,
    )
```

profile of v0, /device:TPU:0, one launch (start us, length us, event | category | flops | bytes accessed | tf_op | source)
XLA Modules:
  0.0 275.7 jit_solution(11968080390307770625)
XLA Ops:
  7.2 0.0 copy-start
  7.2 0.9 compare_bitcast_fusion.1
  8.0 0.9 compare_and_fusion.1
  8.9 1.3 compare_bitcast_fusion.2
  10.2 0.8 copy.86
  11.0 0.8 copy.85
  11.8 0.8 copy.87
  12.5 1.0 reshape.142
  13.6 1.7 bitcast_select_fusion.1
  15.3 3.1 %gather_fusion.1 = bf16[432,256]{1,0:T(8,128)(2,1)} fusion(bf16[256,256]{1,0:T(8,128)(2,1)} %bitcast_select_fusion.1, s32[1024]{0:T(1024)S(1)} %pad_clamp_fusion.2), kind=kCustom, calls=%fused_computation.clone | custom fusion | bytes 444096 | tf_op jit(solution)/shard_map/jit(_take)/gather | solution.py:16
  18.4 1.7 reshape.145
  20.1 2.3 broadcast_select_fusion.3
  22.4 0.8 copy.89
  23.3 1.7 reshape.99
  25.0 0.0 copy-done
  25.0 2.2 fusion.4
  27.2 1.7 reshape.100
  28.9 1.8 copy.90
  30.7 7.3 %all-to-all-start = ((bf16[27,8,2,256]{3,2,0,1:T(2,128)(2,1)}), bf16[27,8,2,256]{3,2,0,1:T(2,128)(2,1)}, u32[]{:S(2)}, u32[]{:S(2)}) async-start(bf16[27,8,2,256]{3,2,0,1:T(2,128)(2,1)} %copy.90), calls=%async_computation | async-start | bytes 442368 | tf_op jit(solution)/shard_map/all_to_all | solution.py:53
  38.0 0.0 reduce-scatter.2.cloned.1.call-start
  38.0 0.0 copy-done.4
  38.0 0.6 compare_bitcast_fusion
  38.6 0.6 compare_and_fusion
  39.2 0.8 broadcast_maximum_fusion
  40.0 0.0 copy-start.3
  40.0 1.4 broadcast_compare_fusion
  41.4 0.0 copy-done.3
  41.4 1.5 copy.102
  42.9 0.8 copy.84
  43.7 0.7 copy.81
  44.4 1.5 copy.101
  45.9 1.4 copy.95
  47.3 1.4 copy.94
  48.8 1.7 reshape.122
  50.5 1.4 pad_clamp_fusion
  51.9 1.5 copy.96
  53.3 1.0 reshape.146
  54.4 1.0 squeeze.16
  55.4 18.5 %gather_fusion = bf16[6912,256]{1,0:T(8,128)(2,1)} fusion(bf16[256,256]{1,0:T(8,128)(2,1)} %bitcast_select_fusion.1, s32[7168]{0:T(1024)} %pad_clamp_fusion), kind=kCustom, calls=%fused_computation.2 | custom fusion | bytes 7105536 | tf_op jit(solution)/shard_map/jit(_take)/gather | solution.py:16
  73.9 6.4 %reshape.121 = bf16[256,27,256]{2,1,0:T(8,128)(2,1)} reshape(bf16[6912,256]{1,0:T(8,128)(2,1)} %gather_fusion) | data formatting | bytes 7077888 | tf_op jit(solution)/shard_map/jit(_take)/gather | solution.py:16
  80.3 7.6 %select_select_fusion = bf16[256,27,256]{2,1,0:T(8,128)(2,1)} fusion(bf16[256,27,256]{2,1,0:T(8,128)(2,1)} %reshape.121, pred[256,27]{1,0:T(8,128)(4,1)} %copy.81, pred[256,27]{1,0:T(8,128)(4,1)} %bitcast.53), kind=kLoop, calls=%fused_computation.5 | loop fusion | flops 3538944 | bytes 7091712 | tf_op jit(solution)/shard_map/jit(_where)/select_n | solution.py:17
  87.9 7.4 %copy.93 = bf16[256,27,256]{0,2,1:T(8,128)(2,1)} copy(bf16[256,27,256]{2,1,0:T(8,128)(2,1)} %select_select_fusion) | data formatting | bytes 7077888 | tf_op jit(solution)/shard_map/jit(_where)/select_n | solution.py:17
  95.3 3.8 %fusion.7 = f32[256,256]{1,0:T(8,128)} fusion(bf16[256,27,256]{0,2,1:T(8,128)(2,1)} %copy.93, bf16[1,27,256,256]{3,2,1,0:T(8,128)(2,1)S(1)} %copy-done), kind=kOutput, calls=%fused_computation.11 | convolution fusion | flops 905969664 | bytes 7340032 | tf_op jit(solution)/shard_map/dot_general | solution.py:33
  99.1 0.0 all-to-all-done
  99.1 1.0 copy_convert_fusion
  100.1 1.0 copy.92
  101.1 2.1 reshape.132
  103.1 4.7 %scatter_fusion = f32[256,256]{1,0:T(8,128)} fusion(f32[256,256]{1,0:T(8,128)} %fusion.7, s32[432]{0:T(512)S(1)} %bitcast.54, f32[432,256]{1,0:T(8,128)} %reshape.132), kind=kCustom, calls=%fused_computation.3 | custom fusion | flops 110592 | bytes 1328832 | tf_op jit(solution)/shard_map/scatter-add | solution.py:65
  107.9 0.0 copy-done.5
  107.9 1.8 bitcast_select_fusion
  109.7 3.1 %gather_fusion.2 = bf16[432,256]{1,0:T(8,128)(2,1)} fusion(bf16[256,256]{1,0:T(8,128)(2,1)} %get-tuple-element.7, s32[1024]{0:T(1024)S(1)} %pad_clamp_fusion.1), kind=kCustom, calls=%fused_computation.1.clone | custom fusion | bytes 444096 | tf_op jit(solution)/shard_map/jit(_take)/gather | solution.py:16
  112.8 1.7 reshape.149
  114.5 2.3 broadcast_select_fusion.2
  116.8 13.7 %all_to_all.10 = bf16[27,8,2,256]{3,2,0,1:T(2,128)(2,1)S(1)} all-to-all(bf16[27,8,2,256]{3,2,0,1:T(2,128)(2,1)S(1)} %broadcast_select_fusion.2), channel_id=1, replica_groups=mesh['section'=4,'space'=8] {'space'}, dimensions={1} | all-to-all | bytes 442368 | tf_op jit(solution)/shard_map/all_to_all | solution.py:54
  130.5 0.8 copy.98
  131.4 1.7 reshape.101
  133.1 2.3 fusion.11
  135.4 0.0 copy-done.1
  135.4 4.0 %add_multiply_fusion = f32[27,256,256]{2,1,0:T(8,128)} fusion(f32[27,256,256]{2,1,0:T(8,128)S(1)} %fusion.11, bf16[256,27,256]{0,2,1:T(8,128)(2,1)S(1)} %copy-done.1, bf16[256,256]{1,0:T(8,128)(2,1)S(1)} %copy-done.2), kind=kOutput, calls=%fused_computation.4 | convolution fusion | flops 909508608 | bytes 17825792 | tf_op jit(solution)/shard_map/dot_general | solution.py:36
  139.4 0.0 reduce-scatter.2.cloned.1.call-update
  139.4 1.3 collective-permute-start
  140.7 2.3 collective-permute-done
  143.0 124.3 %reduce-scatter.2.cloned.1.call-done = f32[864,256]{1,0:T(8,128)} async-done(((f32[6912,256]{1,0:T(8,128)}), f32[864,256]{1,0:T(8,128)}) %reduce-scatter.2.cloned.1.call-update) | async-done | bytes 884752 | tf_op jit(solution)/shard_map/reduce_scatter | solution.py:69
  267.3 1.6 copy.109
  (9 shorter events, 0.0 us)
Async XLA Ops:
  7.2 17.8 %copy-start = (bf16[1,27,256,256]{3,2,1,0:T(8,128)(2,1)S(1)}, bf16[1,27,256,256]{3,2,1,0:T(8,128)(2,1)}, u32[]{:S(2)}) copy-start(bf16[1,27,256,256]{3,2,1,0:T(8,128)(2,1)} %param.11) | copy-start | bytes 10616836
  18.4 19.6 %copy-start.4 = (s32[1,1,27,8,2]{2,4,3,1,0:T(2,128)S(1)}, s32[1,1,27,8,2]{2,4,3,1,0:T(2,128)}, u32[]{:S(2)}) copy-start(s32[1,1,27,8,2]{2,4,3,1,0:T(2,128)} %param.15) | copy-start | bytes 5188
  30.7 68.4 %all-to-all-start = ((bf16[27,8,2,256]{3,2,0,1:T(2,128)(2,1)}), bf16[27,8,2,256]{3,2,0,1:T(2,128)(2,1)}, u32[]{:S(2)}, u32[]{:S(2)}) async-start(bf16[27,8,2,256]{3,2,0,1:T(2,128)(2,1)} %copy.90), calls=%async_computation | async-start | bytes 442368 | tf_op jit(solution)/shard_map/all_to_all | solution.py:53
  38.0 229.4 %reduce-scatter.2.cloned.1.call-start = ((), (), s32[]{:S(2)}) async-start(), calls=%async_computation.3 | async-start | bytes 7962624 | tf_op jit(solution)/shard_map/reduce_scatter | solution.py:69
  40.0 1.4 copy-start.3
  103.1 4.7 %copy-start.5 = (pred[256]{0:T(512)(128)(4,1)S(1)}, pred[256]{0:T(512)(128)(4,1)}, u32[]{:S(2)}) copy-start(pred[256]{0:T(512)(128)(4,1)} %compare_bitcast_fusion.2) | copy-start | bytes 772
  133.1 2.3 copy-start.1
  133.1 2.3 copy-start.2
  139.4 3.6 %collective-permute-start = (bf16[256,256]{1,0:T(8,128)(2,1)}, bf16[256,256]{1,0:T(8,128)(2,1)}, u32[]{:S(2)}, u32[]{:S(2)}) collective-permute-start(bf16[256,256]{1,0:T(8,128)(2,1)} %get-tuple-element.8), channel_id=1, source_target_pairs={{8,0},{16,8},{24,16},{9,1},{17,9},{25,17},{10,2},{18,10},{26,18},{... | collective-permute-start | bytes 393224 | tf_op jit(solution)/shard_map/ppermute | solution.py:12
Sparse Core Ops, SparseCore 0:
  139.6 127.7 reduce-scatter.1
where the time goes:
time: 278 us; the launch traced here: 276 us
  waiting for transfers between devices  127 us (46%)
  local copies, waits for them, and re-layouts  71 us (26%)
  other arithmetic  29.3 us (11%)
  between operations  14.2 us (5%)
  blocking collectives  13.7 us (5%)
  matrix products  12.3 us (4%)
  starting transfers between devices  8.61 us (3%)
    reduce_scatter x1, waiting for transfers between devices, body(): lax.psum_scatter((weight_grad * loss_scale).reshape(offsets * channels, c...  124 us
    gather x6, local copies, waits for them, and re-layouts, take_rows(): picked = jnp.take(source, jnp.maximum(row_index, 0), axis=0)  34.5 us
    all_to_all x1, blocking collectives, body(): lax.all_to_all(take_rows(xmask, recv_map, nothing), 'space', split_axis=1...  13.7 us
    select_n x3, other arithmetic, take_rows(): return jnp.where((row_index >= 0)[..., None], picked, nothing)  12.3 us
    select_n x2, local copies, waits for them, and re-layouts, take_rows(): return jnp.where((row_index >= 0)[..., None], picked, nothing)  8.23 us
    all_to_all x1, starting transfers between devices, body(): lax.all_to_all(partial_value, 'space', split_axis=1, concat_axis=1, tiled...  7.28 us
  transfers between devices with their start and end apart: 3, of which 2 were waited for; matrix products, arithmetic and copies ran while one was open for 22% of the time, Pallas kernels for 0%

commit v1 on v0

--- a/solution.py
+++ b/solution.py
@@ -1,9 +1,46 @@
+import functools
 import jax
 import jax.numpy as jnp
 from jax import lax
 from jax.sharding import PartitionSpec as P
 
 BLOCK = 128
+
+
+def _obtain_quarters(sample, array_dim, mat):
+    val2 = sample.shape
+    built = sample.reshape(*val2[:array_dim], mat, val2[array_dim] // mat, *val2[array_dim + 1 :])
+    return jnp.moveaxis(built, array_dim, 0)
+
+
+def show_gates(inner_x, d_out):
+    inner_x = jnp.moveaxis(inner_x, 0, d_out)
+    current_arr = inner_x.shape
+    return inner_x.reshape(
+        *current_arr[:d_out], current_arr[d_out] * current_arr[d_out + 1], *current_arr[d_out + 2 :]
+    )
+
+
+def obtain_strips_all_on(packet, axis_tag, my_tile, patch):
+    spare, formed = (jax.lax.axis_size(axis_tag), jax.lax.axis_index(axis_tag))
+    extra = _obtain_quarters(packet, my_tile, spare)
+    w = 1
+    known = extra
+    while w < spare:
+        part_next, even = ((formed + w) % spare, (formed - w) % spare)
+        side_arr = lax.dynamic_index_in_dim(extra, part_next, 0)
+        column = []
+        dev_i = 0
+        while dev_i < spare:
+            column.append((dev_i, (dev_i + w) % spare))
+            dev_i = dev_i + 1
+        seen_now = jax.lax.ppermute(side_arr, axis_tag, column)
+        known = lax.dynamic_update_slice_in_dim(known, seen_now, even, axis=0)
+        w += 1
+    return show_gates(known, patch)
+
+
+raise_edge = functools.partial(obtain_strips_all_on, axis_tag="space", my_tile=1, patch=1)
 
 
 def from_behind(block, axis, distance):
@@ -51,9 +88,7 @@
         .reshape(outgoing.shape)
     )
     arrived = lax.all_to_all(partial_value, "space", split_axis=1, concat_axis=1, tiled=True)
-    returned = lax.all_to_all(
-        take_rows(xmask, recv_map, nothing), "space", split_axis=1, concat_axis=1, tiled=True
-    )
+    returned = raise_edge(take_rows(xmask, recv_map, nothing))
     weight_grad = weight_grad + lax.dot_general(
         outgoing.reshape(flat_shape),
         returned.reshape(flat_shape),

time: 278 us -> 291 us (1.047)
  blocking collectives: 13.7 us -> 0 us
  starting transfers between devices: 8.61 us -> 21.2 us
  matrix products: 12.3 us -> 19.3 us
  other arithmetic: 29.3 us -> 33.3 us
    all_to_all x1 -> x0, blocking collectives: 13.7 us -> none  [body(): lax.all_to_all(take_rows(xmask, recv_map, nothing), 'space', split_axis=1...]
    ppermute x0 -> x7, starting transfers between devices: none -> 12.6 us  [obtain_strips_all_on(): seen_now = jax.lax.ppermute(side_arr, axis_tag, column)]
    dot_general x1, matrix products: 2.31 us -> 7.26 us  [body(): lax.dot_general(outgoing.reshape(flat_shape), returned.reshape(flat_shape...]
    dynamic_update_slice x0 -> x7, local copies, waits for them, and re-layouts: none -> 4.4 us  [obtain_strips_all_on(): known = lax.dynamic_update_slice_in_dim(known, seen_now, even, axis=0)]
    select_n x2 -> x1, local copies, waits for them, and re-layouts: 8.23 us -> 7.41 us  [take_rows(): return jnp.where((row_index >= 0)[..., None], picked, nothing)]
  transfers between devices with their start and end apart: 3 -> 10, of which waited for: 2 -> 2; matrix products, arithmetic and copies ran while one was open for 22% -> 24% of each run, Pallas kernels for 0% -> 0%
where the time goes in v1:
time: 291 us; the launch traced here: 289 us
  waiting for transfers between devices  128 us (44%)
  local copies, waits for them, and re-layouts  73.1 us (25%)
  other arithmetic  33.3 us (11%)
  starting transfers between devices  21.2 us (7%)
  matrix products  19.3 us (7%)
  between operations  14.1 us (5%)
    reduce_scatter x1, waiting for transfers between devices, body(): lax.psum_scatter((weight_grad * loss_scale).reshape(offsets * channels, c...  126 us
    gather x6, local copies, waits for them, and re-layouts, take_rows(): picked = jnp.take(source, jnp.maximum(row_index, 0), axis=0)  34.4 us
    ppermute x7, starting transfers between devices, obtain_strips_all_on(): seen_now = jax.lax.ppermute(side_arr, axis_tag, column)  12.6 us
    select_n x3, other arithmetic, take_rows(): return jnp.where((row_index >= 0)[..., None], picked, nothing)  11.5 us
    select_n x1, local copies, waits for them, and re-layouts, take_rows(): return jnp.where((row_index >= 0)[..., None], picked, nothing)  7.41 us
    all_to_all x1, starting transfers between devices, body(): lax.all_to_all(partial_value, 'space', split_axis=1, concat_axis=1, tiled...  7.28 us
    dot_general x1, matrix products, body(): lax.dot_general(outgoing.reshape(flat_shape), returned.reshape(flat_shape...  7.26 us
    dot_general x1, matrix products, body(): lax.dot_general(gathered, xmask, (((0,), (0,)), ((), ())), preferred_elem...  5.95 us
  transfers between devices with their start and end apart: 10, of which 2 were waited for; matrix products, arithmetic and copies ran while one was open for 24% of the time, Pallas kernels for 0%

profile of v1, /device:TPU:0, one launch (start us, length us, event | category | flops | bytes accessed | tf_op | source)
XLA Modules:
  0.0 289.2 jit_solution(18088367469687221452)
XLA Ops:
  7.2 0.9 compare_bitcast_fusion.1
  8.0 0.9 compare_and_fusion.1
  8.9 1.3 compare_bitcast_fusion.2
  10.2 0.8 copy.60
  11.0 0.8 copy.62
  11.8 1.0 reshape.163
  12.8 1.7 bitcast_select_fusion.1
  14.5 3.1 %gather_fusion.1 = bf16[432,256]{1,0:T(8,128)(2,1)} fusion(bf16[256,256]{1,0:T(8,128)(2,1)} %bitcast_select_fusion.1, s32[1024]{0:T(1024)S(1)} %pad_clamp_fusion.2), kind=kCustom, calls=%fused_computation.clone | custom fusion | bytes 444096 | tf_op jit(solution)/shard_map/jit(_take)/gather | solution.py:53
  17.6 1.7 reshape.166
  19.3 0.8 copy.61
  20.0 2.2 broadcast_select_fusion.3
  22.3 1.7 reshape.120
  24.0 2.2 fusion.4
  26.2 1.7 reshape.121
  27.9 1.8 copy.63
  29.7 7.3 %all-to-all-start = ((bf16[27,8,2,256]{3,2,0,1:T(2,128)(2,1)}), bf16[27,8,2,256]{3,2,0,1:T(2,128)(2,1)}, u32[]{:S(2)}, u32[]{:S(2)}) async-start(bf16[27,8,2,256]{3,2,0,1:T(2,128)(2,1)} %copy.63), calls=%async_computation | async-start | bytes 442368 | tf_op jit(solution)/shard_map/all_to_all | solution.py:90
  37.0 1.4 broadcast_maximum_fusion
  38.4 1.5 copy.73
  39.9 0.8 bitcast_compare_fusion
  40.6 1.4 broadcast_compare_fusion
  42.0 0.8 copy.59
  44.0 1.7 reshape.143
  45.7 1.4 pad_clamp_fusion
  47.1 18.5 %gather_fusion = bf16[6912,256]{1,0:T(8,128)(2,1)} fusion(bf16[256,256]{1,0:T(8,128)(2,1)} %bitcast_select_fusion.1, s32[7168]{0:T(1024)} %pad_clamp_fusion), kind=kCustom, calls=%fused_computation.2 | custom fusion | bytes 7105536 | tf_op jit(solution)/shard_map/jit(_take)/gather | solution.py:53
  65.5 6.4 %reshape.142 = bf16[256,27,256]{2,1,0:T(8,128)(2,1)} reshape(bf16[6912,256]{1,0:T(8,128)(2,1)} %gather_fusion) | data formatting | bytes 7077888 | tf_op jit(solution)/shard_map/jit(_take)/gather | solution.py:53
  71.9 0.7 copy.56
  72.6 1.5 copy.72
  74.1 7.7 %select_select_fusion = bf16[256,27,256]{2,1,0:T(8,128)(2,1)} fusion(bf16[256,27,256]{2,1,0:T(8,128)(2,1)} %reshape.142, pred[256,27]{1,0:T(8,128)(4,1)} %copy.56, pred[256,27]{1,0:T(8,128)(4,1)} %bitcast.74), kind=kLoop, calls=%fused_computation.5 | loop fusion | flops 3538944 | bytes 7091712 | tf_op jit(solution)/shard_map/jit(_where)/select_n | solution.py:54
  81.8 7.4 %copy.66 = bf16[256,27,256]{0,2,1:T(8,128)(2,1)} copy(bf16[256,27,256]{2,1,0:T(8,128)(2,1)} %select_select_fusion) | data formatting | bytes 7077888 | tf_op jit(solution)/shard_map/jit(_where)/select_n | solution.py:54
  89.2 1.6 squeeze.16
  90.8 1.3 compare_select_fusion.2
  92.1 0.8 copy.69
  92.9 1.0 reshape.167
  93.9 0.8 copy.68
  94.7 0.8 copy.67
  95.5 3.8 %fusion.7 = f32[256,256]{1,0:T(8,128)} fusion(bf16[256,27,256]{0,2,1:T(8,128)(2,1)} %copy.66, bf16[1,27,256,256]{3,2,1,0:T(8,128)(2,1)S(1)} %copy-done), kind=kOutput, calls=%fused_computation.11 | convolution fusion | flops 905969664 | bytes 7340032 | tf_op jit(solution)/shard_map/dot_general | solution.py:70
  99.3 1.0 copy_convert_fusion
  100.3 1.0 copy.65
  101.3 2.1 reshape.153
  103.4 4.7 %scatter_fusion = f32[256,256]{1,0:T(8,128)} fusion(f32[256,256]{1,0:T(8,128)} %fusion.7, s32[432]{0:T(512)S(1)} %bitcast.75, f32[432,256]{1,0:T(8,128)} %reshape.153), kind=kCustom, calls=%fused_computation.3 | custom fusion | flops 110592 | bytes 1328832 | tf_op jit(solution)/shard_map/scatter-add | solution.py:100
  108.1 1.8 bitcast_select_fusion
  109.9 0.7 copy-done.1
  110.5 5.9 %fusion.10 = f32[27,256,256]{2,1,0:T(8,128)} fusion(bf16[256,27,256]{0,2,1:T(8,128)(2,1)} %copy.66, bf16[256,256]{1,0:T(8,128)(2,1)S(1)} %get-tuple-element.14), kind=kOutput, calls=%fused_computation.18 | convolution fusion | flops 905969664 | bytes 10747904 | tf_op jit(solution)/shard_map/dot_general | solution.py:73
  116.5 3.1 %gather_fusion.2 = bf16[432,256]{1,0:T(8,128)(2,1)} fusion(bf16[256,256]{1,0:T(8,128)(2,1)} %copy-done.1, s32[1024]{0:T(1024)S(1)} %pad_clamp_fusion.1), kind=kCustom, calls=%fused_computation.1.clone | custom fusion | bytes 444096 | tf_op jit(solution)/shard_map/jit(_take)/gather | solution.py:53
  119.6 1.7 reshape.170
  121.3 1.6 broadcast_select_fusion.2
  123.1 2.0 collective-permute-start.1
  125.1 2.2 fusion.17
  127.3 1.5 collective-permute-start.2
  128.8 2.4 collective-permute-start.3
  131.1 1.5 collective-permute-start.4
  132.6 2.4 collective-permute-start.5
  135.0 1.5 collective-permute-start.6
  137.1 1.5 collective-permute-start.7
  139.2 0.6 constant_dynamic-update-slice_fusion.4
  139.8 0.6 constant_dynamic-update-slice_fusion.3
  140.4 0.6 constant_dynamic-update-slice_fusion.2
  141.7 0.6 constant_dynamic-update-slice_fusion
  142.3 1.7 reshape_reshape.3
  144.0 7.3 %add_multiply_fusion = f32[27,256,256]{2,1,0:T(8,128)} fusion(f32[27,256,256]{2,1,0:T(8,128)} %fusion.10, bf16[27,16,256]{2,1,0:T(8,128)(2,1)} %reshape.120, bf16[27,16,256]{2,1,0:T(8,128)(2,1)} %reshape_reshape.3), kind=kOutput, calls=%fused_computation.4 | convolution fusion | flops 60162048 | bytes 14598144 | tf_op jit(solution)/shard_map/dot_general | solution.py:92
  151.3 1.3 collective-permute-start
  152.6 2.3 collective-permute-done
  154.9 125.9 %reduce-scatter.2.cloned.1.call-done = f32[864,256]{1,0:T(8,128)} async-done(((f32[6912,256]{1,0:T(8,128)}), f32[864,256]{1,0:T(8,128)}) %reduce-scatter.2.cloned.1.call-update) | async-done | bytes 884752 | tf_op jit(solution)/shard_map/reduce_scatter | solution.py:104
  280.7 1.6 copy.85
  (33 shorter events, 3.4 us)
Async XLA Ops:
  7.2 16.8 %copy-start = (bf16[1,27,256,256]{3,2,1,0:T(8,128)(2,1)S(1)}, bf16[1,27,256,256]{3,2,1,0:T(8,128)(2,1)}, u32[]{:S(2)}) copy-start(bf16[1,27,256,256]{3,2,1,0:T(8,128)(2,1)} %param.11) | copy-start | bytes 10616836
  17.6 24.4 %copy-start.2 = (s32[1,1,27,8,2]{2,4,3,1,0:T(2,128)S(1)}, s32[1,1,27,8,2]{2,4,3,1,0:T(2,128)}, u32[]{:S(2)}) copy-start(s32[1,1,27,8,2]{2,4,3,1,0:T(2,128)} %param.15) | copy-start | bytes 5188
  29.7 69.6 %all-to-all-start = ((bf16[27,8,2,256]{3,2,0,1:T(2,128)(2,1)}), bf16[27,8,2,256]{3,2,0,1:T(2,128)(2,1)}, u32[]{:S(2)}, u32[]{:S(2)}) async-start(bf16[27,8,2,256]{3,2,0,1:T(2,128)(2,1)} %copy.63), calls=%async_computation | async-start | bytes 442368 | tf_op jit(solution)/shard_map/all_to_all | solution.py:90
  37.0 243.8 %reduce-scatter.2.cloned.1.call-start = ((), (), s32[]{:S(2)}) async-start(), calls=%async_computation.2 | async-start | bytes 7962624 | tf_op jit(solution)/shard_map/reduce_scatter | solution.py:104
  81.8 10.3 %copy-start.3 = (s32[27,8,2]{0,2,1:T(2,128)S(1)}, s32[27,8,2]{0,2,1:T(2,128)}, u32[]{:S(2)}) copy-start(s32[27,8,2]{0,2,1:T(2,128)} %get-tuple-element.4) | copy-start | bytes 5188
  81.8 12.1 %copy-start.5 = (pred[27,8,2]{0,2,1:T(4,128)(4,1)S(1)}, pred[27,8,2]{0,2,1:T(4,128)(4,1)}, u32[]{:S(2)}) copy-start(pred[27,8,2]{0,2,1:T(4,128)(4,1)} %get-tuple-element.3) | copy-start | bytes 1300
  81.8 12.9 %copy-start.4 = (pred[27,8,2]{0,2,1:T(4,128)(4,1)S(1)}, pred[27,8,2]{0,2,1:T(4,128)(4,1)}, u32[]{:S(2)}) copy-start(pred[27,8,2]{0,2,1:T(4,128)(4,1)} %compare_bitcast_fusion) | copy-start | bytes 1300
  95.5 7.9 %copy-start.6 = (s32[432,1]{0,1:T(1,128)S(1)}, s32[432,1]{0,1:T(1,128)}, u32[]{:S(2)}) copy-start(s32[432,1]{0,1:T(1,128)} %compare_select_fusion.2) | copy-start | bytes 5188
  103.4 4.7 %copy-start.7 = (pred[256]{0:T(512)(128)(4,1)S(1)}, pred[256]{0:T(512)(128)(4,1)}, u32[]{:S(2)}) copy-start(pred[256]{0:T(512)(128)(4,1)} %compare_bitcast_fusion.2) | copy-start | bytes 772
  109.9 0.7 copy-start.1
  123.1 11.9 %collective-permute-start.1 = (bf16[1,27,1,2,256]{4,3,0,1,2:T(2,128)(2,1)S(1)}, bf16[1,27,1,2,256]{4,3,0,1,2:T(2,128)(2,1)S(1)}, u32[]{:S(2)}, u32[]{:S(2)}) collective-permute-start(bf16[1,27,1,2,256]{4,3,0,1,2:T(2,128)(2,1)S(1)} %get-tuple-element.13), channel_id=1, source_target_pairs={{0,1},{1,2},{2,3},{3,4},{4,5},{5,6},{6,7},{7,0},{8,9},{9,10},{10,1... | collective-permute-start | bytes 82952 | tf_op jit(solution)/shard_map/ppermute | solution.py:37
  127.3 9.8 %collective-permute-start.2 = (bf16[1,27,1,2,256]{4,3,0,1,2:T(2,128)(2,1)S(1)}, bf16[1,27,1,2,256]{4,3,0,1,2:T(2,128)(2,1)S(1)}, u32[]{:S(2)}, u32[]{:S(2)}) collective-permute-start(bf16[1,27,1,2,256]{4,3,0,1,2:T(2,128)(2,1)S(1)} %get-tuple-element.12), channel_id=1, source_target_pairs={{0,2},{1,3},{2,4},{3,5},{4,6},{5,7},{6,0},{7,1},{8,10},{9,11},{10,... | collective-permute-start | bytes 82952 | tf_op jit(solution)/shard_map/ppermute | solution.py:37
  128.8 10.4 %collective-permute-start.3 = (bf16[1,27,1,2,256]{4,3,0,1,2:T(2,128)(2,1)S(1)}, bf16[1,27,1,2,256]{4,3,0,1,2:T(2,128)(2,1)S(1)}, u32[]{:S(2)}, u32[]{:S(2)}) collective-permute-start(bf16[1,27,1,2,256]{4,3,0,1,2:T(2,128)(2,1)S(1)} %get-tuple-element.11), channel_id=1, source_target_pairs={{0,3},{1,4},{2,5},{3,6},{4,7},{5,0},{6,1},{7,2},{8,11},{9,12},{10,... | collective-permute-start | bytes 82952 | tf_op jit(solution)/shard_map/ppermute | solution.py:37
  131.1 8.6 %collective-permute-start.4 = (bf16[1,27,1,2,256]{4,3,0,1,2:T(2,128)(2,1)S(1)}, bf16[1,27,1,2,256]{4,3,0,1,2:T(2,128)(2,1)S(1)}, u32[]{:S(2)}, u32[]{:S(2)}) collective-permute-start(bf16[1,27,1,2,256]{4,3,0,1,2:T(2,128)(2,1)S(1)} %get-tuple-element.10), channel_id=1, source_target_pairs={{0,4},{1,5},{2,6},{3,7},{4,0},{5,1},{6,2},{7,3},{8,12},{9,13},{10,... | collective-permute-start | bytes 82952 | tf_op jit(solution)/shard_map/ppermute | solution.py:37
  132.6 7.8 %collective-permute-start.5 = (bf16[1,27,1,2,256]{4,3,0,1,2:T(2,128)(2,1)S(1)}, bf16[1,27,1,2,256]{4,3,0,1,2:T(2,128)(2,1)S(1)}, u32[]{:S(2)}, u32[]{:S(2)}) collective-permute-start(bf16[1,27,1,2,256]{4,3,0,1,2:T(2,128)(2,1)S(1)} %get-tuple-element.9), channel_id=1, source_target_pairs={{0,5},{1,6},{2,7},{3,0},{4,1},{5,2},{6,3},{7,4},{8,13},{9,14},{10,... | collective-permute-start | bytes 82952 | tf_op jit(solution)/shard_map/ppermute | solution.py:37
  135.0 6.1 %collective-permute-start.6 = (bf16[1,27,1,2,256]{4,3,0,1,2:T(2,128)(2,1)S(1)}, bf16[1,27,1,2,256]{4,3,0,1,2:T(2,128)(2,1)S(1)}, u32[]{:S(2)}, u32[]{:S(2)}) collective-permute-start(bf16[1,27,1,2,256]{4,3,0,1,2:T(2,128)(2,1)S(1)} %get-tuple-element.8), channel_id=1, source_target_pairs={{0,6},{1,7},{2,0},{3,1},{4,2},{5,3},{6,4},{7,5},{8,14},{9,15},{10,... | collective-permute-start | bytes 82952 | tf_op jit(solution)/shard_map/ppermute | solution.py:37
  137.1 4.6 %collective-permute-start.7 = (bf16[1,27,1,2,256]{4,3,0,1,2:T(2,128)(2,1)S(1)}, bf16[1,27,1,2,256]{4,3,0,1,2:T(2,128)(2,1)S(1)}, u32[]{:S(2)}, u32[]{:S(2)}) collective-permute-start(bf16[1,27,1,2,256]{4,3,0,1,2:T(2,128)(2,1)S(1)} %get-tuple-element.7), channel_id=1, source_target_pairs={{0,7},{1,0},{2,1},{3,2},{4,3},{5,4},{6,5},{7,6},{8,15},{9,8},{10,9... | collective-permute-start | bytes 82952 | tf_op jit(solution)/shard_map/ppermute | solution.py:37
  151.3 3.6 %collective-permute-start = (bf16[256,256]{1,0:T(8,128)(2,1)}, bf16[256,256]{1,0:T(8,128)(2,1)}, u32[]{:S(2)}, u32[]{:S(2)}) collective-permute-start(bf16[256,256]{1,0:T(8,128)(2,1)} %get-tuple-element.15), channel_id=1, source_target_pairs={{8,0},{16,8},{24,16},{9,1},{17,9},{25,17},{10,2},{18,10},{26,18},{... | collective-permute-start | bytes 393224 | tf_op jit(solution)/shard_map/ppermute | solution.py:49
Sparse Core Ops, SparseCore 0:
  151.4 129.2 reduce-scatter.1
